TPU v7x, 32 devices: a whole 2x2x4 slice. The times are simulated.
32 devices in a mesh: groups: 2 (over y), row: 8 (over z, x), col: 2 (over core).
Axes of the slice: x: 2, y: 2, z: 4, core: 2. Of those that a mesh axis runs over, the one named last changes fastest.
Arguments:
- teacher: bfloat16 [16384, 4096], P(('groups', 'row'), 'col'), parts along dimension 0, may hold values from -6 to 6
- proj_weight: bfloat16 [4096, 512], P('col'), may hold values from -0.09375 to 0.09375
- student: bfloat16 [512, 32, 512], P(('groups', 'col'), 'row'), parts along dimension 0, may hold values from -6 to 6
- dw_kernel: float32 [7, 7, 512], replicated, may hold values from -2 to 2
- dw_bias: float32 [512], replicated, may hold values from -4 to 4
- norm_gain: float32 [512], replicated, may hold values from 0.1 to 1.9
- norm_bias: float32 [512], replicated, may hold values from -4 to 4
- w_in: bfloat16 [512, 2048], replicated, may hold values from -0.25 to 0.25
- b_in: float32 [2048], replicated, may hold values from -4 to 4
- w_out: bfloat16 [2048, 512], replicated, may hold values from -0.125 to 0.125
- b_out: float32 [512], replicated, may hold values from -4 to 4
- layer_scale: float32 [512], replicated, may hold values from 0.25 to 1
Outputs:
- student_grad: float32 [512, 32, 512], P(('groups', 'col'), 'row'), parts along dimension 0
There are 2 independent parts, one for each index of `groups`. A program takes and returns all parts, laid end to end along the dimension named above; an argument that names none is the same for every part. Nothing has to cross between parts.
All inputs are finite; a program needn't handle non-finite values.
Results may differ from a plain program's by a relative error of at most 0.0044.
Values may be sent and summed in bfloat16 or wider, within the bound.
No kernel may reach another device: no remote copies, remote signals or barrier semaphores. Data moves between devices by JAX's collectives and lax.ppermute only.
A program may use at most 64 MiB of HBM per device.

v0:
```python
import jax
import jax.numpy as jnp
from jax import lax
from jax.sharding import PartitionSpec as P

NORM_EPSILON = 1e-06


def with_halo(block, sides, width):
    for axis, dim in sides:
        count = lax.axis_size(axis)
        forward = [(i, i + 1) for i in range(count - 1)]
        backward = [(target, source) for source, target in forward]
        low = lax.ppermute(
            lax.slice_in_dim(block, block.shape[dim] - width, None, axis=dim), axis, forward
        )
        high = lax.ppermute(lax.slice_in_dim(block, 0, width, axis=dim), axis, backward)
        block = jnp.concatenate([low, block, high], axis=dim)
    return block


def depthwise(padded, kernel, out_rows, out_cols):
    summed = jnp.zeros((out_rows, out_cols, padded.shape[2]), jnp.float32)
    for row_tap in range(7):
        for col_tap in range(7):
            window = padded[row_tap : row_tap + out_rows, col_tap : col_tap + out_cols].astype(
                jnp.float32
            )
            summed = summed + kernel[row_tap, col_tap] * window
    return summed


def gelu_slope(values):
    return (
        0.5 * (1.0 + lax.erf(values * 0.7071067811865476))
        + values * jnp.exp(-0.5 * values * values) * 0.3989422804014327
    )


def on_device(
    teacher,
    proj_weight,
    student,
    dw_kernel,
    dw_bias,
    norm_gain,
    norm_bias,
    w_in,
    b_in,
    w_out,
    b_out,
    layer_scale,
):
    row_count = lax.axis_size("row")
    tile_v, tile_u, channels = student.shape
    grid_u = tile_u * row_count
    local_lines = teacher.shape[0] // grid_u
    raw_tokens = teacher.reshape(local_lines, grid_u, teacher.shape[1])
    arrived = lax.all_to_all(raw_tokens, "row", split_axis=1, concat_axis=0, tiled=True)
    partial_value = jnp.dot(
        arrived.reshape(-1, arrived.shape[2]), proj_weight, preferred_element_type=jnp.float32
    )
    partial_value = partial_value.reshape(arrived.shape[0], tile_u, channels)
    target = lax.psum_scatter(partial_value, "col", scatter_dimension=0, tiled=True).astype(
        jnp.bfloat16
    )
    padded = with_halo(student, (("row", 1), ("col", 0)), 3)
    conv_out = depthwise(padded, dw_kernel, tile_v, tile_u) + dw_bias
    mean_val = jnp.mean(conv_out, axis=-1, keepdims=True)
    centred = conv_out - mean_val
    variance = jnp.mean(centred * centred, axis=-1, keepdims=True)
    inv_scale = lax.rsqrt(variance + NORM_EPSILON)
    normal_form = centred * inv_scale
    normed = (normal_form * norm_gain + norm_bias).astype(jnp.bfloat16).reshape(-1, channels)
    hidden_pre = jnp.dot(normed, w_in, preferred_element_type=jnp.float32) + b_in
    activated = jax.nn.gelu(hidden_pre, approximate=False).astype(jnp.bfloat16)
    branch = jnp.dot(activated, w_out, preferred_element_type=jnp.float32) + b_out
    branch = branch.reshape(tile_v, tile_u, channels)
    mismatch = student.astype(jnp.float32) + layer_scale * branch - target.astype(jnp.float32)
    d_branch = (layer_scale * mismatch).astype(jnp.bfloat16).reshape(-1, channels)
    d_activated = jnp.dot(d_branch, w_out.T, preferred_element_type=jnp.float32)
    d_hidden = (d_activated * gelu_slope(hidden_pre)).astype(jnp.bfloat16)
    d_normed = jnp.dot(d_hidden, w_in.T, preferred_element_type=jnp.float32).reshape(
        tile_v, tile_u, channels
    )
    scaled = d_normed * norm_gain
    d_conv_out = inv_scale * (
        scaled
        - jnp.mean(scaled, axis=-1, keepdims=True)
        - normal_form * jnp.mean(scaled * normal_form, axis=-1, keepdims=True)
    )
    d_padded = with_halo(d_conv_out, (("row", 1), ("col", 0)), 3)
    return mismatch + depthwise(d_padded, dw_kernel[::-1, ::-1], tile_v, tile_u)


def solution(mesh):
    placed = (
        P(("groups", "row"), "col"),
        P("col", None),
        P(("groups", "col"), "row", None),
        P(),
        P(),
        P(),
        P(),
        P(),
        P(),
        P(),
        P(),
        P(),
    )
    return jax.shard_map(
        on_device,
        mesh=mesh,
        in_specs=placed,
        out_specs=P(("groups", "col"), "row", None),
        check_vma=False,
    )
```

profile of v0, /device:TPU:11, one launch (start us, length us, event | category | flops | bytes accessed | tf_op | source)
XLA Modules:
  0.0 258.3 jit_solution(15804994926780199484)
XLA Ops:
  6.5 6.7 %copy.56 = bf16[32,32,2048]{2,0,1:T(8,128)(2,1)} copy(bf16[32,32,2048]{2,1,0:T(8,128)(2,1)} %bitcast.64) | data formatting | bytes 8388608 | tf_op jit(solution)/shard_map/reshape | solution.py:58
  13.2 5.8 %all-to-all-start = ((bf16[32,32,2048]{2,0,1:T(8,128)(2,1)}), bf16[32,32,2048]{2,0,1:T(8,128)(2,1)}, u32[]{:S(2)}, u32[]{:S(2)}) async-start(bf16[32,32,2048]{2,0,1:T(8,128)(2,1)} %copy.56), calls=%async_computation | async-start | bytes 8388608 | tf_op jit(solution)/shard_map/all_to_all | solution.py:59
  19.5 3.1 %collective-permute-start = (bf16[128,3,512]{2,0,1:T(8,128)(2,1)S(1)}, bf16[128,3,512]{2,0,1:T(8,128)(2,1)S(1)}, u32[]{:S(2)}, u32[]{:S(2)}) collective-permute-start(bf16[128,3,512]{2,0,1:T(8,128)(2,1)S(1)} %copy.80), channel_id=1, source_target_pairs={{0,2},{2,4},{4,6},{6,8},{8,10},{10,12},{12,14},{1,3},{3,5},{5,7},{... | collective-permute-start | bytes 1179656 | tf_op jit(solution)/shard_map/ppermute | solution.py:14
  22.7 2.2 collective-permute-start.1
  25.0 93.0 %collective-permute-done = bf16[128,3,512]{2,0,1:T(8,128)(2,1)S(1)} collective-permute-done((bf16[128,3,512]{2,0,1:T(8,128)(2,1)S(1)}, bf16[128,3,512]{2,0,1:T(8,128)(2,1)S(1)}, u32[]{:S(2)}, u32[]{:S(2)}) %collective-permute-start) | collective-permute-done | bytes 393248 | tf_op jit(solution)/shard_map/ppermute | solution.py:14
  121.9 2.4 collective-permute-start.3
  125.6 2.6 %copy.57 = bf16[8,32,4,2048]{3,1,0,2:T(8,128)(2,1)S(1)} copy(bf16[8,32,4,2048]{3,1,2,0:T(8,128)(2,1)} %bitcast.51) | data formatting | bytes 8388608 | tf_op jit(solution)/shard_map/all_to_all | solution.py:59
  128.5 3.7 %fusion.16 = f32[256,4,512]{2,0,1:T(8,128)} fusion(bf16[256,4,2048]{2,0,1:T(8,128)(2,1)S(1)} %bitcast.65, bf16[2048,512]{1,0:T(8,128)(2,1)S(1)} %copy-done.13), kind=kOutput, calls=%fused_computation.76 | convolution fusion | flops 2147483648 | bytes 8388608 | tf_op jit(solution)/shard_map/dot_general | solution.py:60
  132.2 21.4 %fusion.185 = (f32[128,4]{0,1:T(4,128)S(1)}, f32[128,4,512]{2,0,1:T(8,128)S(1)}) fusion(f32[512]{0:T(512)S(1)} %copy-done.11, bf16[3,10,512]{2,0,1:T(4,128)(2,1)S(1)} %collective-permute-done.3, bf16[128,10,512]{2,0,1:T(8,128)(2,1)} %copy-done.7, f32[512]{0:T(512)S(1)} %bitcast.122, f32[512]{0:T(512)S(1)} %bitcast.124, f32[512]{0:T(512)S(1)} %bitcast.68, ...), kind=kLoop, calls=%fused_computation.343 | loop fusion | flops 71826944 | bytes 6195200 | tf_op jit(solution)/shard_map/reduce_sum | solution.py:69
  155.4 2.0 reshape.52
  157.4 2.4 fusion.193
  159.8 1.9 copy-done.6
  161.8 10.1 %fusion.20 = f32[512,512]{1,0:T(8,128)} fusion(bf16[2048,512]{1,0:T(8,128)(2,1)S(1)} %copy-done.14, f32[512,2048]{1,0:T(8,128)S(1)} %fusion.193, f32[2048]{0:T(1024)S(1)} %copy-done.15, f32[512]{0:T(512)S(1)} %copy-done.16), kind=kOutput, calls=%fused_computation.79 | convolution fusion | flops 1143209984 | bytes 7350272 | tf_op jit(solution)/shard_map/dot_general | solution.py:77
  171.9 2.6 %reshape.53 = f32[128,4,512]{2,1,0:T(4,128)} reshape(f32[512,512]{1,0:T(8,128)} %fusion.20) | data formatting | bytes 2097152 | tf_op jit(solution)/shard_map/reshape | solution.py:78
  174.5 2.1 multiply_convert_fusion
  177.8 2.0 reshape.55
  179.8 7.0 %multiply_reduce_fusion.1 = (f32[512]{0:T(512)S(1)}, f32[512,512]{1,0:T(8,128)}) fusion(f32[512]{0:T(512)S(1)} %copy-done.9, bf16[512,2048]{1,0:T(8,128)(2,1)S(1)} %copy-done, f32[512,2048]{1,0:T(8,128)} %copy-done.6, bf16[512,512]{1,0:T(8,128)(2,1)} %reshape.55, bf16[2048,512]{1,0:T(8,128)(2,1)} %param.21, f32[2048]{0:T(1024)S(1)} %copy-done.15), kind=kOutput, calls=%fused_computation.216 | convolution fusion | flops 2159541760 | bytes 9973760 | tf_op jit(solution)/shard_map/dot_general | solution.py:83
  186.9 2.5 reshape.56
  193.2 1.9 collective-permute-start.5
  195.1 5.0 %collective-permute-start.4 = (f32[128,3,512]{2,0,1:T(8,128)S(1)}, f32[128,3,512]{2,0,1:T(8,128)S(1)}, u32[]{:S(2)}, u32[]{:S(2)}) collective-permute-start(f32[128,3,512]{2,0,1:T(8,128)S(1)} %get-tuple-element.13), channel_id=1, source_target_pairs={{0,2},{2,4},{4,6},{6,8},{8,10},{10,12},{12,14},{1,3},{3,5},{5,7},{... | collective-permute-start | bytes 2359304 | tf_op jit(solution)/shard_map/ppermute | solution.py:14
  200.1 26.2 %collective-permute-done.5 = f32[128,3,512]{2,0,1:T(8,128)S(1)} collective-permute-done((f32[128,3,512]{2,0,1:T(8,128)S(1)}, f32[128,3,512]{2,0,1:T(8,128)S(1)}, u32[]{:S(2)}, u32[]{:S(2)}) %collective-permute-start.5) | collective-permute-done | bytes 786464 | tf_op jit(solution)/shard_map/ppermute | solution.py:17
  226.3 6.7 %collective-permute-done.4 = f32[128,3,512]{2,0,1:T(8,128)S(1)} collective-permute-done((f32[128,3,512]{2,0,1:T(8,128)S(1)}, f32[128,3,512]{2,0,1:T(8,128)S(1)}, u32[]{:S(2)}, u32[]{:S(2)}) %collective-permute-start.4) | collective-permute-done | bytes 786464 | tf_op jit(solution)/shard_map/ppermute | solution.py:14
  234.5 3.0 %collective-permute-start.7 = (f32[3,10,512]{2,0,1:T(4,128)S(1)}, f32[3,10,512]{2,0,1:T(4,128)S(1)}, u32[]{:S(2)}, u32[]{:S(2)}) collective-permute-start(f32[3,10,512]{2,0,1:T(4,128)S(1)} %get-tuple-element.10), channel_id=1, source_target_pairs={{1,0},{3,2},{5,4},{7,6},{9,8},{11,10},{13,12},{15,14},{17,16},{19,... | collective-permute-start | bytes 184328 | tf_op jit(solution)/shard_map/ppermute | solution.py:17
  239.6 10.3 %fusion.85 = f32[128,4,512]{2,0,1:T(8,128)S(1)} fusion(f32[131,10,512]{2,0,1:T(8,128)S(1)} %get-tuple-element.8, f32[128,3,512]{2,0,1:T(8,128)S(1)} %collective-permute-done.5, f32[128,4,512]{2,0,1:T(8,128)S(1)} %subtract_multiply_fusion, f32[128,3,512]{2,0,1:T(8,128)S(1)} %collective-permute-done.4, f32[131,10,512]{2,0,1:T(8,128)S(1)} %get-tuple-element.7, ...), kind=kLoop, calls=%fused_computation.145 | loop fusion | flops 28835840 | bytes 50434048 | tf_op jit(solution)/shard_map/add | solution.py:93
  (70 shorter events, 17.8 us)
Async XLA Ops:
  6.5 150.9 %copy-start = (bf16[512,2048]{1,0:T(8,128)(2,1)S(1)}, bf16[512,2048]{1,0:T(8,128)(2,1)}, u32[]{:S(2)}) copy-start(bf16[512,2048]{1,0:T(8,128)(2,1)} %param.19) | copy-start | bytes 6291460
  13.2 5.8 %copy-start.1 = (bf16[128,4,512]{2,1,0:T(4,128)(2,1)S(1)}, bf16[128,4,512]{2,1,0:T(4,128)(2,1)}, u32[]{:S(2)}) copy-start(bf16[128,4,512]{2,1,0:T(4,128)(2,1)} %param.14) | copy-start | bytes 1572868
  13.2 11.7 %copy-start.8 = (f32[7,7,512]{2,1,0:T(8,128)S(1)}, f32[7,7,512]{2,1,0:T(8,128)}, u32[]{:S(2)}) copy-start(f32[7,7,512]{2,1,0:T(8,128)} %param.15) | copy-start | bytes 301060
  13.2 112.4 %all-to-all-start = ((bf16[32,32,2048]{2,0,1:T(8,128)(2,1)}), bf16[32,32,2048]{2,0,1:T(8,128)(2,1)}, u32[]{:S(2)}, u32[]{:S(2)}) async-start(bf16[32,32,2048]{2,0,1:T(8,128)(2,1)} %copy.56), calls=%async_computation | async-start | bytes 8388608 | tf_op jit(solution)/shard_map/all_to_all | solution.py:59
  19.0 155.5 %reduce-scatter.2.cloned.1.call-start = ((), (), s32[]{:S(2)}) async-start(), calls=%async_computation.2 | async-start | bytes 3145728 | tf_op jit(solution)/shard_map/reduce_scatter | solution.py:64
  19.5 98.5 %collective-permute-start = (bf16[128,3,512]{2,0,1:T(8,128)(2,1)S(1)}, bf16[128,3,512]{2,0,1:T(8,128)(2,1)S(1)}, u32[]{:S(2)}, u32[]{:S(2)}) collective-permute-start(bf16[128,3,512]{2,0,1:T(8,128)(2,1)S(1)} %copy.80), channel_id=1, source_target_pairs={{0,2},{2,4},{4,6},{6,8},{8,10},{10,12},{12,14},{1,3},{3,5},{5,7},{... | collective-permute-start | bytes 1179656 | tf_op jit(solution)/shard_map/ppermute | solution.py:14
  22.7 97.3 %collective-permute-start.1 = (bf16[128,3,512]{2,0,1:T(8,128)(2,1)S(1)}, bf16[128,3,512]{2,0,1:T(8,128)(2,1)S(1)}, u32[]{:S(2)}, u32[]{:S(2)}) collective-permute-start(bf16[128,3,512]{2,0,1:T(8,128)(2,1)S(1)} %copy.81), channel_id=1, source_target_pairs={{2,0},{4,2},{6,4},{8,6},{10,8},{12,10},{14,12},{3,1},{5,3},{7,5},{... | collective-permute-start | bytes 1179656 | tf_op jit(solution)/shard_map/ppermute | solution.py:17
  121.9 10.3 %collective-permute-start.3 = (bf16[3,10,512]{2,0,1:T(4,128)(2,1)S(1)}, bf16[3,10,512]{2,0,1:T(4,128)(2,1)S(1)}, u32[]{:S(2)}, u32[]{:S(2)}) collective-permute-start(bf16[3,10,512]{2,0,1:T(4,128)(2,1)S(1)} %get-tuple-element.12), channel_id=1, source_target_pairs={{1,0},{3,2},{5,4},{7,6},{9,8},{11,10},{13,12},{15,14},{17,16},{19,... | collective-permute-start | bytes 92168 | tf_op jit(solution)/shard_map/ppermute | solution.py:17
  124.3 7.9 %collective-permute-start.2 = (bf16[3,10,512]{2,0,1:T(4,128)(2,1)S(1)}, bf16[3,10,512]{2,0,1:T(4,128)(2,1)S(1)}, u32[]{:S(2)}, u32[]{:S(2)}) collective-permute-start(bf16[3,10,512]{2,0,1:T(4,128)(2,1)S(1)} %get-tuple-element.11), channel_id=1, source_target_pairs={{0,1},{2,3},{4,5},{6,7},{8,9},{10,11},{12,13},{14,15},{16,17},{18,... | collective-permute-start | bytes 92168 | tf_op jit(solution)/shard_map/ppermute | solution.py:14
  125.6 2.9 %copy-start.13 = (bf16[2048,512]{1,0:T(8,128)(2,1)S(1)}, bf16[2048,512]{1,0:T(8,128)(2,1)}, u32[]{:S(2)}) copy-start(bf16[2048,512]{1,0:T(8,128)(2,1)} %param.13) | copy-start | bytes 6291460
  128.5 3.7 %copy-start.11 = (f32[512]{0:T(512)S(1)}, f32[512]{0:T(512)}, u32[]{:S(2)}) copy-start(f32[512]{0:T(512)} %param.16) | copy-start | bytes 6148
  132.2 21.7 %copy-start.9 = (f32[512]{0:T(512)S(1)}, f32[512]{0:T(512)}, u32[]{:S(2)}) copy-start(f32[512]{0:T(512)} %param.17) | copy-start | bytes 6148
  132.2 21.7 %copy-start.12 = (f32[512]{0:T(512)S(1)}, f32[512]{0:T(512)}, u32[]{:S(2)}) copy-start(f32[512]{0:T(512)} %param.18) | copy-start | bytes 6148
  155.4 6.4 %copy-start.15 = (f32[2048]{0:T(1024)S(1)}, f32[2048]{0:T(1024)}, u32[]{:S(2)}) copy-start(f32[2048]{0:T(1024)} %param.20) | copy-start | bytes 24580
  155.4 6.4 %copy-start.16 = (f32[512]{0:T(512)S(1)}, f32[512]{0:T(512)}, u32[]{:S(2)}) copy-start(f32[512]{0:T(512)} %param.22) | copy-start | bytes 6148
  157.4 4.4 %copy-start.14 = (bf16[2048,512]{1,0:T(8,128)(2,1)S(1)}, bf16[2048,512]{1,0:T(8,128)(2,1)}, u32[]{:S(2)}) copy-start(bf16[2048,512]{1,0:T(8,128)(2,1)} %param.21) | copy-start | bytes 6291460
  161.8 12.7 %copy-start.10 = (f32[512]{0:T(512)S(1)}, f32[512]{0:T(512)}, u32[]{:S(2)}) copy-start(f32[512]{0:T(512)} %param.23) | copy-start | bytes 6148
  193.2 33.1 %collective-permute-start.5 = (f32[128,3,512]{2,0,1:T(8,128)S(1)}, f32[128,3,512]{2,0,1:T(8,128)S(1)}, u32[]{:S(2)}, u32[]{:S(2)}) collective-permute-start(f32[128,3,512]{2,0,1:T(8,128)S(1)} %get-tuple-element.14), channel_id=1, source_target_pairs={{2,0},{4,2},{6,4},{8,6},{10,8},{12,10},{14,12},{3,1},{5,3},{7,5},{... | collective-permute-start | bytes 2359304 | tf_op jit(solution)/shard_map/ppermute | solution.py:17
  195.1 37.9 %collective-permute-start.4 = (f32[128,3,512]{2,0,1:T(8,128)S(1)}, f32[128,3,512]{2,0,1:T(8,128)S(1)}, u32[]{:S(2)}, u32[]{:S(2)}) collective-permute-start(f32[128,3,512]{2,0,1:T(8,128)S(1)} %get-tuple-element.13), channel_id=1, source_target_pairs={{0,2},{2,4},{4,6},{6,8},{8,10},{10,12},{12,14},{1,3},{3,5},{5,7},{... | collective-permute-start | bytes 2359304 | tf_op jit(solution)/shard_map/ppermute | solution.py:14
  233.1 6.5 %copy-start.2 = (bf16[128,4,512]{2,1,0:T(4,128)(2,1)S(1)}, bf16[128,4,512]{2,1,0:T(4,128)(2,1)}, u32[]{:S(2)}) copy-start(bf16[128,4,512]{2,1,0:T(4,128)(2,1)} %param.14) | copy-start | bytes 1572868
  233.1 6.5 %copy-start.3 = (f32[128,4,512]{2,1,0:T(4,128)S(1)}, f32[128,4,512]{2,1,0:T(4,128)}, u32[]{:S(2)}) copy-start(f32[128,4,512]{2,1,0:T(4,128)} %reshape.53) | copy-start | bytes 3145732
  233.1 6.5 %copy-start.5 = (f32[128,4,512]{2,0,1:T(8,128)S(1)}, f32[128,4,512]{2,0,1:T(8,128)}, u32[]{:S(2)}) copy-start(f32[128,4,512]{2,0,1:T(8,128)} %reduce-scatter.2.cloned.1.call-done) | copy-start | bytes 3145732
  233.1 4.5 %collective-permute-start.6 = (f32[3,10,512]{2,0,1:T(4,128)S(1)}, f32[3,10,512]{2,0,1:T(4,128)S(1)}, u32[]{:S(2)}, u32[]{:S(2)}) collective-permute-start(f32[3,10,512]{2,0,1:T(4,128)S(1)} %get-tuple-element.9), channel_id=1, source_target_pairs={{0,1},{2,3},{4,5},{6,7},{8,9},{10,11},{12,13},{14,15},{16,17},{18,... | collective-permute-start | bytes 184328 | tf_op jit(solution)/shard_map/ppermute | solution.py:14
  234.5 3.9 %collective-permute-start.7 = (f32[3,10,512]{2,0,1:T(4,128)S(1)}, f32[3,10,512]{2,0,1:T(4,128)S(1)}, u32[]{:S(2)}, u32[]{:S(2)}) collective-permute-start(f32[3,10,512]{2,0,1:T(4,128)S(1)} %get-tuple-element.10), channel_id=1, source_target_pairs={{1,0},{3,2},{5,4},{7,6},{9,8},{11,10},{13,12},{15,14},{17,16},{19,... | collective-permute-start | bytes 184328 | tf_op jit(solution)/shard_map/ppermute | solution.py:17
  (3 other events, 4.0 us)
Sparse Core Ops, SparseCore 0:
  132.3 11.7 reduce-scatter.1
where the time goes:
time: 259 us; the launch traced here: 258 us
  waiting for transfers between devices  127 us (49%)
  other arithmetic  38.8 us (15%)
  local copies, waits for them, and re-layouts  29.6 us (11%)
  starting transfers between devices  26.2 us (10%)
  matrix products  23.3 us (9%)
  between operations  13.8 us (5%)
    ppermute x4, waiting for transfers between devices, with_halo(): lax.ppermute(lax.slice_in_dim(block, block.shape[dim] - width, None, axis...  99.7 us
    ppermute x4, waiting for transfers between devices, with_halo(): lax.ppermute(lax.slice_in_dim(block, 0, width, axis=dim), axis, backward)  27.1 us
    reduce_sum x1, other arithmetic, on_device(): mean_val = jnp.mean(conv_out, axis=-1, keepdims=True)  21.4 us
    ppermute x4, starting transfers between devices, with_halo(): lax.ppermute(lax.slice_in_dim(block, block.shape[dim] - width, None, axis...  10.8 us
    add x1, other arithmetic, on_device(): return mismatch + depthwise(d_padded, dw_kernel[::-1, ::-1], tile_v, tile_u)  10.3 us
    dot_general x1, matrix products, on_device(): jnp.dot(activated, w_out, preferred_element_type=jnp.float32) + b_out  10.1 us
    ppermute x4, starting transfers between devices, with_halo(): lax.ppermute(lax.slice_in_dim(block, 0, width, axis=dim), axis, backward)  9.55 us
    dot_general x1, matrix products, on_device(): jnp.dot(d_hidden, w_in.T, preferred_element_type=jnp.float32)  7.04 us
  transfers between devices with their start and end apart: 10, of which 4 were waited for; matrix products, arithmetic and copies ran while one was open for 19% of the time, Pallas kernels for 0%

commit v1 on v0

--- a/solution.py
+++ b/solution.py
@@ -56,7 +56,10 @@
     grid_u = tile_u * row_count
     local_lines = teacher.shape[0] // grid_u
     raw_tokens = teacher.reshape(local_lines, grid_u, teacher.shape[1])
-    arrived = lax.all_to_all(raw_tokens, "row", split_axis=1, concat_axis=0, tiled=True)
+    s_next = lax.all_to_all(
+        jnp.stack(jnp.split(raw_tokens, lax.axis_size("row"), 1), axis=0), "row", 0, 0
+    )
+    arrived = jnp.concatenate(s_next, 0)
     partial_value = jnp.dot(
         arrived.reshape(-1, arrived.shape[2]), proj_weight, preferred_element_type=jnp.float32
     )

time: 259 us -> 264 us (1.019)
  local copies, waits for them, and re-layouts: 29.6 us -> 34.9 us
    unnamed x37 -> x46, local copies, waits for them, and re-layouts: 4.47 us -> 11.7 us
    reshape x1 -> x0, local copies, waits for them, and re-layouts: 6.67 us -> none  [on_device(): raw_tokens = teacher.reshape(local_lines, grid_u, teacher.shape[1])]
    another operation x0 -> x2, local copies, waits for them, and re-layouts: none -> 4.77 us  [on_device(): jnp.stack(jnp.split(raw_tokens, lax.axis_size('row'), 1), axis=0)]
where the time goes in v1:
time: 264 us
  waiting for transfers between devices  127 us (48%)
  other arithmetic  38.5 us (15%)
  local copies, waits for them, and re-layouts  34.9 us (13%)
  starting transfers between devices  26.2 us (10%)
  matrix products  23.3 us (9%)
  between operations  13.8 us (5%)
    ppermute x4, waiting for transfers between devices, with_halo(): lax.ppermute(lax.slice_in_dim(block, block.shape[dim] - width, None, axis...  99.8 us
    ppermute x4, waiting for transfers between devices, with_halo(): lax.ppermute(lax.slice_in_dim(block, 0, width, axis=dim), axis, backward)  27 us
    reduce_sum x1, other arithmetic, on_device(): mean_val = jnp.mean(conv_out, axis=-1, keepdims=True)  21.2 us
    unnamed x46, local copies, waits for them, and re-layouts  11.7 us
    ppermute x4, starting transfers between devices, with_halo(): lax.ppermute(lax.slice_in_dim(block, block.shape[dim] - width, None, axis...  10.8 us
    add x1, other arithmetic, on_device(): return mismatch + depthwise(d_padded, dw_kernel[::-1, ::-1], tile_v, tile_u)  10.3 us
    dot_general x1, matrix products, on_device(): jnp.dot(activated, w_out, preferred_element_type=jnp.float32) + b_out  10.1 us
    ppermute x4, starting transfers between devices, with_halo(): lax.ppermute(lax.slice_in_dim(block, 0, width, axis=dim), axis, backward)  9.55 us
  transfers between devices with their start and end apart: 10, of which 4 were waited for; matrix products, arithmetic and copies ran while one was open for 19% of the time, Pallas kernels for 0%

profile of v1, /device:TPU:11, one launch (start us, length us, event | category | flops | bytes accessed | tf_op | source)
XLA Modules:
  0.0 263.6 jit_solution(5399488344864434957)
XLA Ops:
  14.2 4.4 %copy.70 = bf16[8,32,4,2048]{3,1,2,0:T(8,128)(2,1)} copy(bf16[8,32,4,2048]{3,2,1,0:T(4,128)(2,1)S(1)} %fusion.150) | data formatting | bytes 8388608 | tf_op jit(solution)/shard_map/stack | solution.py:60
  18.6 5.8 %all-to-all-start = ((bf16[8,32,4,2048]{3,1,2,0:T(8,128)(2,1)}), bf16[8,32,4,2048]{3,1,2,0:T(8,128)(2,1)}, u32[]{:S(2)}, u32[]{:S(2)}) async-start(bf16[8,32,4,2048]{3,1,2,0:T(8,128)(2,1)} %copy.70), calls=%async_computation | async-start | bytes 8388608 | tf_op jit(solution)/shard_map/all_to_all | solution.py:59
  24.9 3.1 %collective-permute-start = (bf16[128,3,512]{2,0,1:T(8,128)(2,1)S(1)}, bf16[128,3,512]{2,0,1:T(8,128)(2,1)S(1)}, u32[]{:S(2)}, u32[]{:S(2)}) collective-permute-start(bf16[128,3,512]{2,0,1:T(8,128)(2,1)S(1)} %copy.94), channel_id=1, source_target_pairs={{0,2},{2,4},{4,6},{6,8},{8,10},{10,12},{12,14},{1,3},{3,5},{5,7},{... | collective-permute-start | bytes 1179656 | tf_op jit(solution)/shard_map/ppermute | solution.py:14
  28.1 2.2 collective-permute-start.1
  30.4 93.0 %collective-permute-done = bf16[128,3,512]{2,0,1:T(8,128)(2,1)S(1)} collective-permute-done((bf16[128,3,512]{2,0,1:T(8,128)(2,1)S(1)}, bf16[128,3,512]{2,0,1:T(8,128)(2,1)S(1)}, u32[]{:S(2)}, u32[]{:S(2)}) %collective-permute-start) | collective-permute-done | bytes 393248 | tf_op jit(solution)/shard_map/ppermute | solution.py:14
  127.3 2.4 collective-permute-start.3
  131.1 2.6 %copy.71 = bf16[8,32,4,2048]{3,1,0,2:T(8,128)(2,1)S(1)} copy(bf16[8,32,4,2048]{3,1,2,0:T(8,128)(2,1)} %all-to-all-done) | data formatting | bytes 8388608 | tf_op jit(solution)/shard_map/all_to_all | solution.py:59
  133.9 3.7 %fusion.16 = f32[256,4,512]{2,0,1:T(8,128)} fusion(bf16[256,4,2048]{2,0,1:T(8,128)(2,1)S(1)} %bitcast.101, bf16[2048,512]{1,0:T(8,128)(2,1)S(1)} %copy-done.14), kind=kOutput, calls=%fused_computation.76 | convolution fusion | flops 2147483648 | bytes 8388608 | tf_op jit(solution)/shard_map/dot_general | solution.py:63
  137.7 21.2 %fusion.193 = (f32[128,4]{0,1:T(4,128)S(1)}, f32[128,4,512]{2,0,1:T(8,128)S(1)}) fusion(f32[512]{0:T(512)S(1)} %copy-done.12, bf16[3,10,512]{2,0,1:T(4,128)(2,1)S(1)} %collective-permute-done.3, bf16[128,10,512]{2,0,1:T(8,128)(2,1)} %copy-done.8, f32[512]{0:T(512)S(1)} %bitcast.158, f32[512]{0:T(512)S(1)} %bitcast.160, f32[512]{0:T(512)S(1)} %bitcast.104, ...), kind=kLoop, calls=%fused_computation.359 | loop fusion | flops 71826944 | bytes 6195200 | tf_op jit(solution)/shard_map/reduce_sum | solution.py:72
  160.6 2.0 reshape.50
  162.6 2.4 fusion.201
  165.1 1.9 copy-done.7
  167.0 10.1 %fusion.20 = f32[512,512]{1,0:T(8,128)} fusion(bf16[2048,512]{1,0:T(8,128)(2,1)S(1)} %copy-done.15, f32[512,2048]{1,0:T(8,128)S(1)} %fusion.201, f32[2048]{0:T(1024)S(1)} %copy-done.16, f32[512]{0:T(512)S(1)} %copy-done.17), kind=kOutput, calls=%fused_computation.79 | convolution fusion | flops 1143209984 | bytes 7350272 | tf_op jit(solution)/shard_map/dot_general | solution.py:80
  177.1 2.6 reshape.51
  179.8 2.1 multiply_convert_fusion
  183.1 2.0 reshape.53
  185.0 7.0 %multiply_reduce_fusion.1 = (f32[512]{0:T(512)S(1)}, f32[512,512]{1,0:T(8,128)}) fusion(f32[512]{0:T(512)S(1)} %copy-done.10, bf16[512,2048]{1,0:T(8,128)(2,1)S(1)} %copy-done, f32[512,2048]{1,0:T(8,128)} %copy-done.7, bf16[512,512]{1,0:T(8,128)(2,1)} %reshape.53, bf16[2048,512]{1,0:T(8,128)(2,1)} %param.21, f32[2048]{0:T(1024)S(1)} %copy-done.16), kind=kOutput, calls=%fused_computation.216 | convolution fusion | flops 2159541760 | bytes 9973760 | tf_op jit(solution)/shard_map/dot_general | solution.py:86
  192.1 2.5 reshape.54
  198.4 1.9 collective-permute-start.5
  200.3 5.0 %collective-permute-start.4 = (f32[128,3,512]{2,0,1:T(8,128)S(1)}, f32[128,3,512]{2,0,1:T(8,128)S(1)}, u32[]{:S(2)}, u32[]{:S(2)}) collective-permute-start(f32[128,3,512]{2,0,1:T(8,128)S(1)} %get-tuple-element.13), channel_id=1, source_target_pairs={{0,2},{2,4},{4,6},{6,8},{8,10},{10,12},{12,14},{1,3},{3,5},{5,7},{... | collective-permute-start | bytes 2359304 | tf_op jit(solution)/shard_map/ppermute | solution.py:14
  205.3 26.1 %collective-permute-done.5 = f32[128,3,512]{2,0,1:T(8,128)S(1)} collective-permute-done((f32[128,3,512]{2,0,1:T(8,128)S(1)}, f32[128,3,512]{2,0,1:T(8,128)S(1)}, u32[]{:S(2)}, u32[]{:S(2)}) %collective-permute-start.5) | collective-permute-done | bytes 786464 | tf_op jit(solution)/shard_map/ppermute | solution.py:17
  231.5 6.8 %collective-permute-done.4 = f32[128,3,512]{2,0,1:T(8,128)S(1)} collective-permute-done((f32[128,3,512]{2,0,1:T(8,128)S(1)}, f32[128,3,512]{2,0,1:T(8,128)S(1)}, u32[]{:S(2)}, u32[]{:S(2)}) %collective-permute-start.4) | collective-permute-done | bytes 786464 | tf_op jit(solution)/shard_map/ppermute | solution.py:14
  239.8 3.0 %collective-permute-start.7 = (f32[3,10,512]{2,0,1:T(4,128)S(1)}, f32[3,10,512]{2,0,1:T(4,128)S(1)}, u32[]{:S(2)}, u32[]{:S(2)}) collective-permute-start(f32[3,10,512]{2,0,1:T(4,128)S(1)} %get-tuple-element.10), channel_id=1, source_target_pairs={{1,0},{3,2},{5,4},{7,6},{9,8},{11,10},{13,12},{15,14},{17,16},{19,... | collective-permute-start | bytes 184328 | tf_op jit(solution)/shard_map/ppermute | solution.py:17
  244.8 10.3 %fusion.85 = f32[128,4,512]{2,0,1:T(8,128)S(1)} fusion(f32[131,10,512]{2,0,1:T(8,128)S(1)} %get-tuple-element.8, f32[128,3,512]{2,0,1:T(8,128)S(1)} %collective-permute-done.5, f32[128,4,512]{2,0,1:T(8,128)S(1)} %subtract_multiply_fusion, f32[128,3,512]{2,0,1:T(8,128)S(1)} %collective-permute-done.4, f32[131,10,512]{2,0,1:T(8,128)S(1)} %get-tuple-element.7, ...), kind=kLoop, calls=%fused_computation.145 | loop fusion | flops 28835840 | bytes 50434048 | tf_op jit(solution)/shard_map/add | solution.py:96
  (80 shorter events, 25.4 us)
Async XLA Ops:
  6.5 156.1 %copy-start = (bf16[512,2048]{1,0:T(8,128)(2,1)S(1)}, bf16[512,2048]{1,0:T(8,128)(2,1)}, u32[]{:S(2)}) copy-start(bf16[512,2048]{1,0:T(8,128)(2,1)} %param.19) | copy-start | bytes 6291460
  6.5 6.4 %copy-start.5 = (bf16[1024,2048]{1,0:T(8,128)(2,1)S(1)}, bf16[1024,2048]{1,0:T(8,128)(2,1)}, u32[]{:S(2)}) copy-start(bf16[1024,2048]{1,0:T(8,128)(2,1)} %param.12) | copy-start | bytes 12582916
  18.6 5.8 %copy-start.1 = (bf16[128,4,512]{2,1,0:T(4,128)(2,1)S(1)}, bf16[128,4,512]{2,1,0:T(4,128)(2,1)}, u32[]{:S(2)}) copy-start(bf16[128,4,512]{2,1,0:T(4,128)(2,1)} %param.14) | copy-start | bytes 1572868
  18.6 11.7 %copy-start.9 = (f32[7,7,512]{2,1,0:T(8,128)S(1)}, f32[7,7,512]{2,1,0:T(8,128)}, u32[]{:S(2)}) copy-start(f32[7,7,512]{2,1,0:T(8,128)} %param.15) | copy-start | bytes 301060
  18.6 112.4 %all-to-all-start = ((bf16[8,32,4,2048]{3,1,2,0:T(8,128)(2,1)}), bf16[8,32,4,2048]{3,1,2,0:T(8,128)(2,1)}, u32[]{:S(2)}, u32[]{:S(2)}) async-start(bf16[8,32,4,2048]{3,1,2,0:T(8,128)(2,1)} %copy.70), calls=%async_computation | async-start | bytes 8388608 | tf_op jit(solution)/shard_map/all_to_all | solution.py:59
  24.4 155.3 %reduce-scatter.2.cloned.1.call-start = ((), (), s32[]{:S(2)}) async-start(), calls=%async_computation.2 | async-start | bytes 3145728 | tf_op jit(solution)/shard_map/reduce_scatter | solution.py:67
  24.9 98.5 %collective-permute-start = (bf16[128,3,512]{2,0,1:T(8,128)(2,1)S(1)}, bf16[128,3,512]{2,0,1:T(8,128)(2,1)S(1)}, u32[]{:S(2)}, u32[]{:S(2)}) collective-permute-start(bf16[128,3,512]{2,0,1:T(8,128)(2,1)S(1)} %copy.94), channel_id=1, source_target_pairs={{0,2},{2,4},{4,6},{6,8},{8,10},{10,12},{12,14},{1,3},{3,5},{5,7},{... | collective-permute-start | bytes 1179656 | tf_op jit(solution)/shard_map/ppermute | solution.py:14
  28.1 97.3 %collective-permute-start.1 = (bf16[128,3,512]{2,0,1:T(8,128)(2,1)S(1)}, bf16[128,3,512]{2,0,1:T(8,128)(2,1)S(1)}, u32[]{:S(2)}, u32[]{:S(2)}) collective-permute-start(bf16[128,3,512]{2,0,1:T(8,128)(2,1)S(1)} %copy.95), channel_id=1, source_target_pairs={{2,0},{4,2},{6,4},{8,6},{10,8},{12,10},{14,12},{3,1},{5,3},{7,5},{... | collective-permute-start | bytes 1179656 | tf_op jit(solution)/shard_map/ppermute | solution.py:17
  127.3 10.3 %collective-permute-start.3 = (bf16[3,10,512]{2,0,1:T(4,128)(2,1)S(1)}, bf16[3,10,512]{2,0,1:T(4,128)(2,1)S(1)}, u32[]{:S(2)}, u32[]{:S(2)}) collective-permute-start(bf16[3,10,512]{2,0,1:T(4,128)(2,1)S(1)} %get-tuple-element.12), channel_id=1, source_target_pairs={{1,0},{3,2},{5,4},{7,6},{9,8},{11,10},{13,12},{15,14},{17,16},{19,... | collective-permute-start | bytes 92168 | tf_op jit(solution)/shard_map/ppermute | solution.py:17
  129.7 7.9 %collective-permute-start.2 = (bf16[3,10,512]{2,0,1:T(4,128)(2,1)S(1)}, bf16[3,10,512]{2,0,1:T(4,128)(2,1)S(1)}, u32[]{:S(2)}, u32[]{:S(2)}) collective-permute-start(bf16[3,10,512]{2,0,1:T(4,128)(2,1)S(1)} %get-tuple-element.11), channel_id=1, source_target_pairs={{0,1},{2,3},{4,5},{6,7},{8,9},{10,11},{12,13},{14,15},{16,17},{18,... | collective-permute-start | bytes 92168 | tf_op jit(solution)/shard_map/ppermute | solution.py:14
  133.9 3.8 %copy-start.12 = (f32[512]{0:T(512)S(1)}, f32[512]{0:T(512)}, u32[]{:S(2)}) copy-start(f32[512]{0:T(512)} %param.16) | copy-start | bytes 6148
  137.6 21.5 %copy-start.10 = (f32[512]{0:T(512)S(1)}, f32[512]{0:T(512)}, u32[]{:S(2)}) copy-start(f32[512]{0:T(512)} %param.17) | copy-start | bytes 6148
  137.6 21.5 %copy-start.13 = (f32[512]{0:T(512)S(1)}, f32[512]{0:T(512)}, u32[]{:S(2)}) copy-start(f32[512]{0:T(512)} %param.18) | copy-start | bytes 6148
  160.6 6.4 %copy-start.16 = (f32[2048]{0:T(1024)S(1)}, f32[2048]{0:T(1024)}, u32[]{:S(2)}) copy-start(f32[2048]{0:T(1024)} %param.20) | copy-start | bytes 24580
  160.6 6.4 %copy-start.17 = (f32[512]{0:T(512)S(1)}, f32[512]{0:T(512)}, u32[]{:S(2)}) copy-start(f32[512]{0:T(512)} %param.22) | copy-start | bytes 6148
  162.6 4.4 %copy-start.15 = (bf16[2048,512]{1,0:T(8,128)(2,1)S(1)}, bf16[2048,512]{1,0:T(8,128)(2,1)}, u32[]{:S(2)}) copy-start(bf16[2048,512]{1,0:T(8,128)(2,1)} %param.21) | copy-start | bytes 6291460
  167.0 12.7 %copy-start.11 = (f32[512]{0:T(512)S(1)}, f32[512]{0:T(512)}, u32[]{:S(2)}) copy-start(f32[512]{0:T(512)} %param.23) | copy-start | bytes 6148
  198.4 33.1 %collective-permute-start.5 = (f32[128,3,512]{2,0,1:T(8,128)S(1)}, f32[128,3,512]{2,0,1:T(8,128)S(1)}, u32[]{:S(2)}, u32[]{:S(2)}) collective-permute-start(f32[128,3,512]{2,0,1:T(8,128)S(1)} %get-tuple-element.14), channel_id=1, source_target_pairs={{2,0},{4,2},{6,4},{8,6},{10,8},{12,10},{14,12},{3,1},{5,3},{7,5},{... | collective-permute-start | bytes 2359304 | tf_op jit(solution)/shard_map/ppermute | solution.py:17
  200.3 38.0 %collective-permute-start.4 = (f32[128,3,512]{2,0,1:T(8,128)S(1)}, f32[128,3,512]{2,0,1:T(8,128)S(1)}, u32[]{:S(2)}, u32[]{:S(2)}) collective-permute-start(f32[128,3,512]{2,0,1:T(8,128)S(1)} %get-tuple-element.13), channel_id=1, source_target_pairs={{0,2},{2,4},{4,6},{6,8},{8,10},{10,12},{12,14},{1,3},{3,5},{5,7},{... | collective-permute-start | bytes 2359304 | tf_op jit(solution)/shard_map/ppermute | solution.py:14
  238.3 6.5 %copy-start.2 = (bf16[128,4,512]{2,1,0:T(4,128)(2,1)S(1)}, bf16[128,4,512]{2,1,0:T(4,128)(2,1)}, u32[]{:S(2)}) copy-start(bf16[128,4,512]{2,1,0:T(4,128)(2,1)} %param.14) | copy-start | bytes 1572868
  238.3 6.5 %copy-start.3 = (f32[128,4,512]{2,1,0:T(4,128)S(1)}, f32[128,4,512]{2,1,0:T(4,128)}, u32[]{:S(2)}) copy-start(f32[128,4,512]{2,1,0:T(4,128)} %reshape.51) | copy-start | bytes 3145732
  238.3 6.5 %copy-start.6 = (f32[128,4,512]{2,0,1:T(8,128)S(1)}, f32[128,4,512]{2,0,1:T(8,128)}, u32[]{:S(2)}) copy-start(f32[128,4,512]{2,0,1:T(8,128)} %reduce-scatter.2.cloned.1.call-done) | copy-start | bytes 3145732
  238.3 4.5 %collective-permute-start.6 = (f32[3,10,512]{2,0,1:T(4,128)S(1)}, f32[3,10,512]{2,0,1:T(4,128)S(1)}, u32[]{:S(2)}, u32[]{:S(2)}) collective-permute-start(f32[3,10,512]{2,0,1:T(4,128)S(1)} %get-tuple-element.9), channel_id=1, source_target_pairs={{0,1},{2,3},{4,5},{6,7},{8,9},{10,11},{12,13},{14,15},{16,17},{18,... | collective-permute-start | bytes 184328 | tf_op jit(solution)/shard_map/ppermute | solution.py:14
  239.8 3.9 %collective-permute-start.7 = (f32[3,10,512]{2,0,1:T(4,128)S(1)}, f32[3,10,512]{2,0,1:T(4,128)S(1)}, u32[]{:S(2)}, u32[]{:S(2)}) collective-permute-start(f32[3,10,512]{2,0,1:T(4,128)S(1)} %get-tuple-element.10), channel_id=1, source_target_pairs={{1,0},{3,2},{5,4},{7,6},{9,8},{11,10},{13,12},{15,14},{17,16},{19,... | collective-permute-start | bytes 184328 | tf_op jit(solution)/shard_map/ppermute | solution.py:17
  (4 other events, 6.9 us)
Sparse Core Ops, SparseCore 0:
  137.7 11.7 reduce-scatter.1
